TPU v7x, 256 devices: a whole 4x4x8 slice. The times are simulated.
256 devices in a mesh: dp: 32 (over z, y_lo, core), mp: 8 (over y_hi, x).
Axes of the slice: x: 4, y: 4 (y_hi: 2, y_lo: 2; y = y_hi * 2 + y_lo), z: 8, core: 2. Of those that a mesh axis runs over, the one named last changes fastest.
Arguments:
- upper_first: bfloat16 [8192, 4096], P('dp'), may hold values from -6 to 6
- upper_second: bfloat16 [8192, 4096], P('dp'), may hold values from -24 to 24
- grad_first: bfloat16 [8192, 4096], P('dp'), may hold values from -6 to 6
- grad_second: bfloat16 [8192, 4096], P('dp'), may hold values from -6 to 6
- norm_gain: bfloat16 [4096], replicated, may hold values from 0.25 to 1.75
- up_weight: bfloat16 [4096, 11264], P('dp', 'mp'), may hold values from -0.09375 to 0.09375
- down_weight: bfloat16 [4096, 11264], P('dp', 'mp'), may hold values from -0.0546875 to 0.0546875
- adapter_down: bfloat16 [4096, 64], replicated, may hold values from -0.09375 to 0.09375
- adapter_up: bfloat16 [64, 4096], replicated, may hold values from -0.75 to 0.75
Outputs:
- lower_first: bfloat16 [8192, 4096], P('dp', 'mp')
- lower_second: bfloat16 [8192, 4096], P('dp', 'mp')
- input_grad_first: bfloat16 [8192, 4096], P('dp', 'mp')
- input_grad_second: bfloat16 [8192, 4096], P('dp')
- adapter_down_grad: float32 [4096, 64], P('mp')
- adapter_up_grad: float32 [64, 4096], P(None, 'mp')
All inputs are finite; a program needn't handle non-finite values.
Results may differ from a plain program's by a relative error of at most 0.009.
Values may be sent and summed in bfloat16 or wider, within the bound.
A program may use at most 128 MiB of HBM per device.

v0:
```python
import math
import jax
import jax.numpy as jnp
from jax import lax
from jax.sharding import PartitionSpec as P

coupling = 0.5


def silu_slope(argument):
    sigmoid_value = jax.nn.sigmoid(argument)
    return sigmoid_value * (1.0 + argument * (1.0 - sigmoid_value))


def on_device(
    upper_first,
    upper_second,
    grad_first,
    grad_second,
    norm_gain,
    up_weight,
    down_weight,
    adapter_down,
    adapter_up,
):
    groups = lax.axis_size("mp")
    mp_rank = lax.axis_index("mp")
    model_width = upper_first.shape[1]
    share_width = model_width // groups
    offset = mp_rank * share_width
    tokens_all = upper_first.shape[0] * lax.axis_size("dp")
    grad_scale = 1.0 / math.sqrt(tokens_all)
    up_full = lax.all_gather(up_weight, "dp", axis=0, tiled=True)
    pre_adapter = jnp.dot(upper_first, adapter_down, preferred_element_type=jnp.float32)
    squashed = jax.nn.silu(pre_adapter).astype(jnp.bfloat16)
    adapted = jnp.dot(squashed, adapter_up, preferred_element_type=jnp.float32)
    lower_full = (upper_second.astype(jnp.float32) - adapted).astype(jnp.bfloat16)
    lower_value = lower_full.astype(jnp.float32)
    inverse_rms = lax.rsqrt(jnp.mean(lower_value * lower_value, axis=1, keepdims=True) + 1e-05)
    gain_full = norm_gain.astype(jnp.float32)
    normed = (lower_value * inverse_rms * gain_full).astype(jnp.bfloat16)
    hidden_pre = jnp.dot(normed, up_full, preferred_element_type=jnp.float32)
    activated = jax.nn.silu(hidden_pre).astype(jnp.bfloat16)
    down_full = lax.all_gather(down_weight, "dp", axis=0, tiled=True)
    partial_out = lax.dot_general(
        activated, down_full, (((1,), (1,)), ((), ())), preferred_element_type=jnp.float32
    )
    frozen_share = lax.psum_scatter(
        partial_out.astype(jnp.bfloat16), "mp", scatter_dimension=1, tiled=True
    ).astype(jnp.float32)
    upper_slice = lax.dynamic_slice_in_dim(upper_first, offset, share_width, 1)
    lower_first = ((upper_slice.astype(jnp.float32) - frozen_share) / coupling).astype(jnp.bfloat16)
    adapter_slope = jnp.einsum(
        "td,rd->tr", grad_second, adapter_up, preferred_element_type=jnp.float32
    )
    adapter_pre_grad = (adapter_slope * silu_slope(pre_adapter)).astype(jnp.bfloat16)
    back_adapter = jnp.einsum(
        "tr,dr->td", adapter_pre_grad, adapter_down, preferred_element_type=jnp.float32
    )
    carried = (grad_first.astype(jnp.float32) + back_adapter).astype(jnp.bfloat16)
    carried_slice = lax.dynamic_slice_in_dim(carried, offset, share_width, 1)
    input_grad_first = (coupling * carried_slice.astype(jnp.float32)).astype(jnp.bfloat16)
    down_grad_part = (
        jnp.einsum("td,tr->dr", upper_slice, adapter_pre_grad, preferred_element_type=jnp.float32)
        * grad_scale
    )
    second_slice = lax.dynamic_slice_in_dim(grad_second, offset, share_width, 1)
    up_grad_part = (
        jnp.einsum("tr,td->rd", squashed, second_slice, preferred_element_type=jnp.float32)
        * grad_scale
    )
    adapter_down_grad, adapter_up_grad = lax.psum((down_grad_part, up_grad_part), "dp")
    act_grad = jnp.dot(carried, down_full, preferred_element_type=jnp.float32)
    pre_grad = (act_grad * silu_slope(hidden_pre)).astype(jnp.bfloat16)
    normed_part = lax.dot_general(
        pre_grad, up_full, (((1,), (1,)), ((), ())), preferred_element_type=jnp.float32
    )
    stat_part = jnp.sum(hidden_pre * pre_grad.astype(jnp.float32), axis=1)
    normed_grad, curvature = lax.psum((normed_part, stat_part), "mp")
    correction = lower_value * inverse_rms * inverse_rms * curvature[:, None] / model_width
    input_grad_second = (
        grad_second.astype(jnp.float32) + inverse_rms * gain_full * normed_grad - correction
    ).astype(jnp.bfloat16)
    lower_second = lax.dynamic_slice_in_dim(lower_full, offset, share_width, 1)
    return (
        lower_first,
        lower_second,
        input_grad_first,
        input_grad_second,
        adapter_down_grad,
        adapter_up_grad,
    )


def solution(mesh):
    return jax.shard_map(
        on_device,
        mesh=mesh,
        in_specs=(
            P("dp", None),
            P("dp", None),
            P("dp", None),
            P("dp", None),
            P(),
            P("dp", "mp"),
            P("dp", "mp"),
            P(),
            P(),
        ),
        out_specs=(
            P("dp", "mp"),
            P("dp", "mp"),
            P("dp", "mp"),
            P("dp", None),
            P("mp", None),
            P(None, "mp"),
        ),
        check_vma=False,
    )
```

profile of v0, /device:TPU:1, one launch (start us, length us, event | category | flops | bytes accessed | tf_op | source)
XLA Modules:
  0.0 618.4 jit_solution(9565982590470995360)
XLA Ops:
  7.2 0.0 copy-start
  7.2 0.0 all-gather.3.cloned.1.call-start
  7.2 0.7 all-gather.3.cloned.1.call-update
  7.9 0.0 all-gather.5.cloned.1.call-start
  8.0 0.7 all-gather.5.cloned.1.call-update
  8.7 0.0 all-reduce.4.cloned.1.call-start
  8.7 0.0 copy-start.5
  8.7 0.8 convert_element_type.65
  9.6 2.4 fusion.22
  12.0 0.0 copy-done
  12.0 0.0 copy-done.5
  12.0 0.0 copy-start.1
  12.0 2.2 fusion.9
  14.3 0.0 copy-start.2
  14.3 0.0 copy-start.3
  14.3 0.0 copy-done.1
  14.3 0.8 fusion.15
  15.0 0.8 copy-done.2
  15.8 0.1 copy-done.3
  15.9 2.1 fusion.1
  18.0 72.4 %all-gather.3.cloned.1.call-done = bf16[4096,1408]{1,0:T(8,128)(2,1)} async-done(((bf16[128,1408]{1,0:T(8,128)(2,1)}), bf16[4096,1408]{1,0:T(8,128)(2,1)}) %all-gather.3.cloned.1.call-update) | async-done | bytes 11534352 | tf_op jit(solution)/shard_map/all_gather | solution.py:33
  90.4 9.6 %fusion.11 = f32[256,1408]{1,0:T(8,128)} fusion(bf16[4096,1408]{1,0:T(8,128)(2,1)} %all-gather.3.cloned.1.call-done, bf16[256,4096]{1,0:T(8,128)(2,1)} %get-tuple-element.9, f32[4096]{0:T(1024)S(1)} %convert_element_type.65, f32[256]{0:T(256)S(1)} %add_rsqrt_fusion), kind=kOutput, calls=%fused_computation.17 | convolution fusion | flops 2956984320 | bytes 15090688 | tf_op jit(solution)/shard_map/dot_general | solution.py:42
  99.9 67.4 %all-gather.5.cloned.1.call-done = bf16[4096,1408]{1,0:T(8,128)(2,1)} async-done(((bf16[128,1408]{1,0:T(8,128)(2,1)}), bf16[4096,1408]{1,0:T(8,128)(2,1)}) %all-gather.5.cloned.1.call-update) | async-done | bytes 11534352 | tf_op jit(solution)/shard_map/all_gather | solution.py:44
  167.3 0.0 copy-start.4
  167.3 9.0 %multiply_reduce_fusion = (f32[256]{0:T(256)S(1)}, bf16[256,1408]{1,0:T(8,128)(2,1)S(1)}) fusion(f32[256,1408]{1,0:T(8,128)} %fusion.11, bf16[256,4096]{1,0:T(8,128)(2,1)} %fusion.1, bf16[4096,1408]{1,0:T(8,128)(2,1)} %all-gather.5.cloned.1.call-done), kind=kOutput, calls=%fused_computation.20 | convolution fusion | flops 2957115136 | bytes 15795200 | tf_op jit(solution)/shard_map/dot_general | solution.py:73
  176.3 0.0 copy-done.4
  176.3 5.0 fusion.23
  181.3 0.0 all-reduce.4.cloned.1.call-update
  181.4 0.2 reduce-scatter.2.cloned.1.call-start
  181.6 9.6 %convolution_convert_fusion = bf16[256,4096]{1,0:T(8,128)(2,1)} fusion(bf16[4096,1408]{1,0:T(8,128)(2,1)} %all-gather.5.cloned.1.call-done, f32[256,1408]{1,0:T(8,128)} %fusion.11), kind=kOutput, calls=%fused_computation.6 | convolution fusion | flops 2955640832 | bytes 15073280 | tf_op jit(solution)/shard_map/dot_general | solution.py:45
  191.1 0.0 reduce-scatter.2.cloned.1.call-update
  191.2 0.0 all-reduce.6.cloned.1.call-start
  191.2 1.8 convolution_multiply_fusion.1
  193.0 0.8 convolution_multiply_fusion.2
  193.9 0.0 all-reduce.6.cloned.1.call-update
  193.9 1.7 constant_dynamic-slice_fusion
  195.6 1.7 multiply_convert_fusion.2
  197.2 21.3 %psum.29 = f32[256]{0:T(256)S(1)} all-reduce(f32[256]{0:T(256)S(1)} %get-tuple-element.10), channel_id=1, replica_groups=mesh['dp'=32,'mp'=8] {'mp'}, use_global_device_ids=true, to_apply=%region_4.5 | all-reduce | flops 256 | bytes 2048 | tf_op jit(solution)/shard_map/psum | solution.py:79
  218.5 76.4 %all-reduce.4.cloned.1.call-done = f32[256,4096]{1,0:T(8,128)} async-done(((f32[256,4096]{1,0:T(8,128)}), f32[256,4096]{1,0:T(8,128)}) %all-reduce.4.cloned.1.call-update) | async-done | bytes 4194320 | tf_op jit(solution)/shard_map/psum | solution.py:79
  294.9 5.8 fusion.8
  300.7 77.4 %reduce-scatter.2.cloned.1.call-done = bf16[256,512]{1,0:T(8,128)(2,1)} async-done(((bf16[256,4096]{1,0:T(8,128)(2,1)}), bf16[256,512]{1,0:T(8,128)(2,1)}) %reduce-scatter.2.cloned.1.call-update) | async-done | bytes 262160 | tf_op jit(solution)/shard_map/reduce_scatter | solution.py:48
  378.1 1.8 multiply_convert_fusion.3
  379.9 228.8 %all-reduce.6.cloned.1.call-done = (f32[512,64]{0,1:T(8,128)}, f32[64,512]{1,0:T(8,128)}) async-done(((f32[512,64]{0,1:T(8,128)}, f32[64,512]{1,0:T(8,128)}), (f32[512,64]{0,1:T(8,128)}, f32[64,512]{1,0:T(8,128)})) %all-reduce.6.cloned.1.call-update) | async-done | bytes 262160 | tf_op jit(solution)/shard_map/psum | solution.py:72
  608.8 1.6 copy.18
  610.4 1.6 copy.19
  (1 shorter events, 0.0 us)
Async XLA Ops:
  7.2 4.8 copy-start
  7.2 83.2 %all-gather.3.cloned.1.call-start = ((), (), s32[]{:S(2)}) async-start(), calls=%async_computation.1 | async-start | bytes 11894784 | tf_op jit(solution)/shard_map/all_gather | solution.py:33
  7.9 159.4 %all-gather.5.cloned.1.call-start = ((), (), s32[]{:S(2)}) async-start(), calls=%async_computation.2 | async-start | bytes 11894784 | tf_op jit(solution)/shard_map/all_gather | solution.py:44
  8.7 286.3 %all-reduce.4.cloned.1.call-start = ((), (), s32[]{:S(2)}) async-start(), calls=%async_computation.4 | async-start | bytes 8388608 | tf_op jit(solution)/shard_map/psum | solution.py:79
  8.7 3.3 copy-start.5
  12.0 2.2 copy-start.1
  14.3 1.6 copy-start.2
  14.3 1.7 copy-start.3
  167.3 9.0 %copy-start.4 = (bf16[4096,1408]{1,0:T(8,128)(2,1)S(1)}, bf16[4096,1408]{1,0:T(8,128)(2,1)}, u32[]{:S(2)}) copy-start(bf16[4096,1408]{1,0:T(8,128)(2,1)} %all-gather.3.cloned.1.call-done) | copy-start | bytes 34603012
  181.4 196.8 %reduce-scatter.2.cloned.1.call-start = ((), (), s32[]{:S(2)}) async-start(), calls=%async_computation.3 | async-start | bytes 2359296 | tf_op jit(solution)/shard_map/reduce_scatter | solution.py:48
  191.2 417.6 %all-reduce.6.cloned.1.call-start = ((), (), s32[]{:S(2)}) async-start(), calls=%async_computation.5 | async-start | bytes 524288 | tf_op jit(solution)/shard_map/psum | solution.py:72
Sparse Core Ops, SparseCore 0:
  9.8 80.4 all-gather.2
  92.2 75.0 all-gather.4
  181.5 113.4 all-reduce.3
  298.9 79.2 reduce-scatter.1
  381.2 227.5 all-reduce.5
where the time goes:
time: 619 us; the launch traced here: 618 us
  waiting for transfers between devices  524 us (85%)
  matrix products  43.3 us (7%)
  blocking collectives  21.3 us (3%)
  between operations  13.9 us (2%)
  other arithmetic  10.2 us (2%)
    psum x1, waiting for transfers between devices, on_device(): lax.psum((down_grad_part, up_grad_part), 'dp')  229 us
    reduce_scatter x1, waiting for transfers between devices, on_device(): lax.psum_scatter(partial_out.astype(jnp.bfloat16), 'mp', scatter_dimensio...  77.4 us
    psum x1, waiting for transfers between devices, on_device(): normed_grad, curvature = lax.psum((normed_part, stat_part), 'mp')  76.4 us
    all_gather x1, waiting for transfers between devices, on_device(): up_full = lax.all_gather(up_weight, 'dp', axis=0, tiled=True)  72.4 us
    all_gather x1, waiting for transfers between devices, on_device(): down_full = lax.all_gather(down_weight, 'dp', axis=0, tiled=True)  67.4 us
    psum x1, blocking collectives, on_device(): normed_grad, curvature = lax.psum((normed_part, stat_part), 'mp')  21.3 us
  transfers between devices with their start and end apart: 5, of which 5 were waited for; matrix products, arithmetic and copies ran while one was open for 7% of the time, Pallas kernels for 0%

commit v1 on v0

--- a/solution.py
+++ b/solution.py
@@ -41,7 +41,9 @@
     normed = (lower_value * inverse_rms * gain_full).astype(jnp.bfloat16)
     hidden_pre = jnp.dot(normed, up_full, preferred_element_type=jnp.float32)
     activated = jax.nn.silu(hidden_pre).astype(jnp.bfloat16)
-    down_full = lax.all_gather(down_weight, "dp", axis=0, tiled=True)
+    down_full = jnp.concatenate(
+        lax.all_to_all(jnp.stack([down_weight] * lax.axis_size("dp")), "dp", 0, 0), axis=0
+    )
     partial_out = lax.dot_general(
         activated, down_full, (((1,), (1,)), ((), ())), preferred_element_type=jnp.float32
     )

time: 619 us -> 789 us (1.27)
  waiting for transfers between devices: 524 us -> 676 us
  starting transfers between devices: 0.38 us -> 11.8 us
    all_gather x1, waiting for transfers between devices: 72.4 us -> 220 us  [on_device(): up_full = lax.all_gather(up_weight, 'dp', axis=0, tiled=True)]
    all_to_all x0 -> x1, waiting for transfers between devices: none -> 68.7 us  [on_device(): lax.all_to_all(jnp.stack([down_weight] * lax.axis_size('dp')), 'dp', 0, 0)]
    all_gather x1 -> x0, waiting for transfers between devices: 67.4 us -> none  [on_device(): down_full = lax.all_gather(down_weight, 'dp', axis=0, tiled=True)]
    all_to_all x0 -> x1, starting transfers between devices: none -> 11.4 us  [on_device(): lax.all_to_all(jnp.stack([down_weight] * lax.axis_size('dp')), 'dp', 0, 0)]
  transfers between devices with their start and end apart: 5 -> 5, of which waited for: 5 -> 5; matrix products, arithmetic and copies ran while one was open for 7% -> 6% of each run, Pallas kernels for 0% -> 0%
where the time goes in v1:
time: 789 us; the launch traced here: 788 us
  waiting for transfers between devices  676 us (86%)
  matrix products  41.5 us (5%)
  blocking collectives  22.3 us (3%)
  between operations  13.9 us (2%)
  local copies, waits for them, and re-layouts  13.1 us (2%)
  starting transfers between devices  11.8 us (1%)
  other arithmetic  9.33 us (1%)
    psum x1, waiting for transfers between devices, on_device(): lax.psum((down_grad_part, up_grad_part), 'dp')  229 us
    all_gather x1, waiting for transfers between devices, on_device(): up_full = lax.all_gather(up_weight, 'dp', axis=0, tiled=True)  220 us
    psum x1, waiting for transfers between devices, on_device(): normed_grad, curvature = lax.psum((normed_part, stat_part), 'mp')  80.6 us
    reduce_scatter x1, waiting for transfers between devices, on_device(): lax.psum_scatter(partial_out.astype(jnp.bfloat16), 'mp', scatter_dimensio...  77.5 us
    all_to_all x1, waiting for transfers between devices, on_device(): lax.all_to_all(jnp.stack([down_weight] * lax.axis_size('dp')), 'dp', 0, 0)  68.7 us
    psum x1, blocking collectives, on_device(): normed_grad, curvature = lax.psum((normed_part, stat_part), 'mp')  22.3 us
  transfers between devices with their start and end apart: 5, of which 5 were waited for; matrix products, arithmetic and copies ran while one was open for 6% of the time, Pallas kernels for 0%

profile of v1, /device:TPU:1, one launch (start us, length us, event | category | flops | bytes accessed | tf_op | source)
XLA Modules:
  0.0 788.2 jit_solution(3163067554819196616)
XLA Ops:
  7.2 0.0 copy-start
  7.2 0.0 all-gather.2.cloned.1.call-start
  7.2 0.7 all-gather.2.cloned.1.call-update
  7.9 6.6 stack.2
  14.5 0.0 copy-start.5
  14.5 0.0 copy-start.2
  14.5 0.0 copy-start.4
  14.5 11.4 %all-to-all-start = ((bf16[32,128,1408]{2,1,0:T(8,128)(2,1)}), bf16[32,128,1408]{2,1,0:T(8,128)(2,1)}, u32[]{:S(2)}, u32[]{:S(2)}) async-start(bf16[32,128,1408]{2,1,0:T(8,128)(2,1)} %stack.2), calls=%async_computation | async-start | bytes 23068672 | tf_op jit(solution)/shard_map/all_to_all | solution.py:45
  26.0 0.0 all-reduce.4.cloned.1.call-start
  26.0 0.0 copy-done.5
  26.0 0.0 copy-start.7
  26.0 0.0 copy-done.2
  26.1 0.0 copy-done.4
  26.1 0.8 fusion.22
  26.8 0.0 copy-done
  26.8 0.8 copy-done.7
  27.6 0.0 copy-start.1
  27.6 2.2 fusion.9
  29.8 0.0 copy-start.3
  29.8 0.0 copy-done.1
  29.9 0.8 fusion.15
  30.6 0.9 copy-done.3
  31.5 2.1 fusion.1
  33.6 219.9 %all-gather.2.cloned.1.call-done = bf16[4096,1408]{1,0:T(8,128)(2,1)} async-done(((bf16[128,1408]{1,0:T(8,128)(2,1)}), bf16[4096,1408]{1,0:T(8,128)(2,1)}) %all-gather.2.cloned.1.call-update) | async-done | bytes 11534352 | tf_op jit(solution)/shard_map/all_gather | solution.py:33
  253.4 9.5 %fusion.11 = f32[256,1408]{1,0:T(8,128)} fusion(bf16[4096,1408]{1,0:T(8,128)(2,1)} %all-gather.2.cloned.1.call-done, bf16[256,4096]{1,0:T(8,128)(2,1)} %get-tuple-element.9, f32[4096]{0:T(1024)S(1)} %convert_element_type.65, f32[256]{0:T(256)S(1)} %add_rsqrt_fusion), kind=kOutput, calls=%fused_computation.17 | convolution fusion | flops 2956984320 | bytes 15090688 | tf_op jit(solution)/shard_map/dot_general | solution.py:42
  263.0 68.7 %all-to-all-done = bf16[32,128,1408]{2,1,0:T(8,128)(2,1)} async-done(((bf16[32,128,1408]{2,1,0:T(8,128)(2,1)}), bf16[32,128,1408]{2,1,0:T(8,128)(2,1)}, u32[]{:S(2)}, u32[]{:S(2)}) %all-to-all-start) | async-done | bytes 11534368 | tf_op jit(solution)/shard_map/all_to_all | solution.py:45
  331.7 0.0 copy-start.6
  331.7 9.0 %multiply_reduce_fusion = (f32[256]{0:T(256)S(1)}, bf16[256,1408]{1,0:T(8,128)(2,1)S(1)}) fusion(f32[256,1408]{1,0:T(8,128)} %fusion.11, bf16[256,4096]{1,0:T(8,128)(2,1)} %fusion.1, bf16[4096,1408]{1,0:T(8,128)(2,1)} %bitcast), kind=kOutput, calls=%fused_computation.20 | convolution fusion | flops 2957115136 | bytes 15795200 | tf_op jit(solution)/shard_map/dot_general | solution.py:75
  340.7 0.0 copy-done.6
  340.7 5.0 fusion.23
  345.8 0.0 all-reduce.4.cloned.1.call-update
  345.8 0.2 reduce-scatter.2.cloned.1.call-start
  346.0 9.5 %convolution_convert_fusion = bf16[256,4096]{1,0:T(8,128)(2,1)} fusion(bf16[4096,1408]{1,0:T(8,128)(2,1)} %bitcast, f32[256,1408]{1,0:T(8,128)} %fusion.11), kind=kOutput, calls=%fused_computation.6 | convolution fusion | flops 2955640832 | bytes 15073280 | tf_op jit(solution)/shard_map/dot_general | solution.py:47
  355.5 0.0 reduce-scatter.2.cloned.1.call-update
  355.6 0.0 all-reduce.6.cloned.1.call-start
  355.6 1.8 convolution_multiply_fusion.1
  357.4 0.8 convolution_multiply_fusion.2
  358.2 0.0 all-reduce.6.cloned.1.call-update
  358.3 1.7 constant_dynamic-slice_fusion
  359.9 1.7 multiply_convert_fusion.2
  361.6 22.3 %psum.29 = f32[256]{0:T(256)S(1)} all-reduce(f32[256]{0:T(256)S(1)} %get-tuple-element.10), channel_id=1, replica_groups=mesh['dp'=32,'mp'=8] {'mp'}, use_global_device_ids=true, to_apply=%region_4.5 | all-reduce | flops 256 | bytes 2048 | tf_op jit(solution)/shard_map/psum | solution.py:81
  383.9 80.6 %all-reduce.4.cloned.1.call-done = f32[256,4096]{1,0:T(8,128)} async-done(((f32[256,4096]{1,0:T(8,128)}), f32[256,4096]{1,0:T(8,128)}) %all-reduce.4.cloned.1.call-update) | async-done | bytes 4194320 | tf_op jit(solution)/shard_map/psum | solution.py:81
  464.5 5.8 fusion.8
  470.3 77.5 %reduce-scatter.2.cloned.1.call-done = bf16[256,512]{1,0:T(8,128)(2,1)} async-done(((bf16[256,4096]{1,0:T(8,128)(2,1)}), bf16[256,512]{1,0:T(8,128)(2,1)}) %reduce-scatter.2.cloned.1.call-update) | async-done | bytes 262160 | tf_op jit(solution)/shard_map/reduce_scatter | solution.py:50
  547.9 1.8 multiply_convert_fusion.3
  549.7 228.8 %all-reduce.6.cloned.1.call-done = (f32[512,64]{0,1:T(8,128)}, f32[64,512]{1,0:T(8,128)}) async-done(((f32[512,64]{0,1:T(8,128)}, f32[64,512]{1,0:T(8,128)}), (f32[512,64]{0,1:T(8,128)}, f32[64,512]{1,0:T(8,128)})) %all-reduce.6.cloned.1.call-update) | async-done | bytes 262160 | tf_op jit(solution)/shard_map/psum | solution.py:74
  778.5 1.6 copy.18
  780.1 1.6 copy.19
  (2 shorter events, 0.0 us)
Async XLA Ops:
  7.2 19.7 %copy-start = (bf16[64,4096]{1,0:T(8,128)(2,1)S(1)}, bf16[64,4096]{1,0:T(8,128)(2,1)}, u32[]{:S(2)}) copy-start(bf16[64,4096]{1,0:T(8,128)(2,1)} %param.17) | copy-start | bytes 1572868
  7.2 246.2 %all-gather.2.cloned.1.call-start = ((), (), s32[]{:S(2)}) async-start(), calls=%async_computation.2 | async-start | bytes 11894784 | tf_op jit(solution)/shard_map/all_gather | solution.py:33
  14.5 11.5 %copy-start.5 = (bf16[4096]{0:T(1024)(128)(2,1)S(1)}, bf16[4096]{0:T(1024)(128)(2,1)}, u32[]{:S(2)}) copy-start(bf16[4096]{0:T(1024)(128)(2,1)} %param.13) | copy-start | bytes 24580
  14.5 11.5 %copy-start.2 = (bf16[256,4096]{1,0:T(8,128)(2,1)S(1)}, bf16[256,4096]{1,0:T(8,128)(2,1)}, u32[]{:S(2)}) copy-start(bf16[256,4096]{1,0:T(8,128)(2,1)} %param.9) | copy-start | bytes 6291460
  14.5 11.5 %copy-start.4 = (bf16[4096,64]{0,1:T(8,128)(2,1)S(1)}, bf16[4096,64]{0,1:T(8,128)(2,1)}, u32[]{:S(2)}) copy-start(bf16[4096,64]{0,1:T(8,128)(2,1)} %param.16) | copy-start | bytes 1572868
  14.5 317.2 %all-to-all-start = ((bf16[32,128,1408]{2,1,0:T(8,128)(2,1)}), bf16[32,128,1408]{2,1,0:T(8,128)(2,1)}, u32[]{:S(2)}, u32[]{:S(2)}) async-start(bf16[32,128,1408]{2,1,0:T(8,128)(2,1)} %stack.2), calls=%async_computation | async-start | bytes 23068672 | tf_op jit(solution)/shard_map/all_to_all | solution.py:45
  26.0 438.6 %all-reduce.4.cloned.1.call-start = ((), (), s32[]{:S(2)}) async-start(), calls=%async_computation.4 | async-start | bytes 8388608 | tf_op jit(solution)/shard_map/psum | solution.py:81
  26.0 1.6 copy-start.7
  27.6 2.2 copy-start.1
  29.8 1.7 copy-start.3
  331.7 9.0 %copy-start.6 = (bf16[4096,1408]{1,0:T(8,128)(2,1)S(1)}, bf16[4096,1408]{1,0:T(8,128)(2,1)}, u32[]{:S(2)}) copy-start(bf16[4096,1408]{1,0:T(8,128)(2,1)} %all-gather.2.cloned.1.call-done) | copy-start | bytes 34603012
  345.8 202.1 %reduce-scatter.2.cloned.1.call-start = ((), (), s32[]{:S(2)}) async-start(), calls=%async_computation.3 | async-start | bytes 2359296 | tf_op jit(solution)/shard_map/reduce_scatter | solution.py:50
  355.6 423.0 %all-reduce.6.cloned.1.call-start = ((), (), s32[]{:S(2)}) async-start(), calls=%async_computation.5 | async-start | bytes 524288 | tf_op jit(solution)/shard_map/psum | solution.py:74
Sparse Core Ops, SparseCore 0:
  9.8 243.5 all-gather.1
  345.9 118.5 all-reduce.3
  468.6 79.2 reduce-scatter.1
  551.0 227.5 all-reduce.5
